TPU v7x, 32 devices: a whole 2x2x4 slice. The times are simulated.
32 devices in a mesh: wide: 8 (over z, y), narrow: 4 (over x, core).
Axes of the slice: x: 2, y: 2, z: 4, core: 2. Of those that a mesh axis runs over, the one named last changes fastest.
Arguments:
- prior_lt: float32 [4096, 6144], P('narrow', 'wide'), may hold values from -2 to 2
- prior_d: float32 [4096], P('narrow'), may hold values from -4 to 4
- prior_e: float32 [4096], P('narrow'), may hold values from -4 to 4
- prior_pairs: int32 [4096], P('narrow'), may hold values from 0 to 1, as said below
- pivots: int32 [2, 256], replicated, may hold values from 0 to 6143, as said below
- a_first: float32 [256, 6144], P('narrow', 'wide'), may hold values from -6 to 6
- a_second: float32 [256, 6144], P('narrow', 'wide'), may hold values from -6 to 6
- inv_d: float32 [2, 256], P(None, 'narrow'), may hold values from -4 to 4
- inv_e: float32 [2, 256], P(None, 'narrow'), may hold values from -4 to 4
- panel_pairs: int32 [2, 256], P(None, 'narrow'), may hold values from 0 to 1, as said below
Outputs:
- l_first: float32 [256, 6144], P('narrow', 'wide')
- l_second: float32 [256, 6144], P('narrow', 'wide')
Inputs may be any that keep to these rules, and one draw needn't show every extreme that they name: `pivots`: all 512 pivot rows are distinct; at most 128 of them lie in one tile of 768 consecutive rows, and some tile holds exactly 128. `prior_pairs`: 1 only at even positions; a 1 at position k joins k and k + 1 into a 2 x 2 pivot block. `panel_pairs`: 1 only at even positions along the last dimension; a 1 at position k joins k and k + 1 into a 2 x 2 pivot block.
All inputs are finite; a program needn't handle non-finite values.
Results may differ from a plain program's by a relative error of at most 0.000098.
Values sent between devices are 32-bit elements; how exact they have to be, the bound alone decides.
A program may use at most 64 MiB of HBM per device.

v0:
```python
import jax
import jax.numpy as jnp
from jax import lax
from jax.sharding import PartitionSpec as P

P_SIZE = 256


def couple(block, diag, off, pairs):
    joined = off * pairs.astype(jnp.float32)
    zero_row = jnp.zeros_like(block[:1])
    after = jnp.concatenate([block[1:], zero_row], 0)
    before = jnp.concatenate([zero_row, block[:-1]], 0)
    lower = jnp.concatenate([jnp.zeros_like(joined[:1]), joined[:-1]], 0)
    return diag[:, None] * block + joined[:, None] * after + lower[:, None] * before


def slot_layout(targets, tile_rows, capacity):
    owner = targets // tile_rows
    count = targets.shape[0]
    order = jnp.arange(count)
    same = (owner[:, None] == owner[None, :]) & (order[:, None] > order[None, :])
    rank = jnp.sum(same.astype(jnp.int32), axis=1)
    return (owner, rank, owner * capacity + rank)


def pack_local(block, targets, owner, rank, here, tile_rows, capacity):
    hit = (owner[None, :] == here) & (rank[None, :] == jnp.arange(capacity)[:, None])
    local_index = jnp.sum(jnp.where(hit, (targets % tile_rows)[None, :], 0), axis=1)
    valid = jnp.any(hit, axis=1)
    taken = jnp.take(block, local_index, axis=1)
    return jnp.where(valid[None, :], taken, 0.0)


def shards(
    prior_lt, prior_d, prior_e, prior_pairs, pivots, a_first, a_second, inv_d, inv_e, panel_pairs
):
    k_local, tile_rows = prior_lt.shape
    blocks = a_first.shape[0]
    narrow_count = lax.axis_size("narrow")
    here = lax.axis_index("wide")
    capacity = max(4 * P_SIZE // lax.axis_size("wide"), 2)
    flat = pivots.reshape(-1)
    second = pivots[1]
    owner, rank, slot = slot_layout(flat, tile_rows, capacity)
    packed = pack_local(prior_lt, flat, owner, rank, here, tile_rows, capacity)
    gathered = lax.all_gather(packed, "wide", axis=1, tiled=True)
    chosen = jnp.take(gathered, slot, axis=1)
    coupled = couple(chosen, prior_d, prior_e, prior_pairs)
    arranged = (
        coupled.reshape(k_local, 2, narrow_count, blocks)
        .transpose(0, 2, 1, 3)
        .reshape(k_local, 2 * P_SIZE)
    )
    columns = arranged
    update = lax.psum_scatter(
        lax.dot_general(
            columns, prior_lt, (((0,), (0,)), ((), ())), precision=lax.Precision.HIGHEST
        ),
        "narrow",
        scatter_dimension=0,
        tiled=True,
    )
    w_first = a_first - update[:blocks]
    l_first = couple(w_first, inv_d[0], inv_e[0], panel_pairs[0])
    owner_two, rank_two, slot_two = slot_layout(second, tile_rows, capacity)
    packed_two = pack_local(l_first, second, owner_two, rank_two, here, tile_rows, capacity)
    gathered_two = lax.all_gather(packed_two, "wide", axis=1, tiled=True)
    crossed = jnp.take(gathered_two, slot_two, axis=1)
    columns = crossed
    correction = lax.psum_scatter(
        lax.dot_general(
            columns, w_first, (((0,), (0,)), ((), ())), precision=lax.Precision.HIGHEST
        ),
        "narrow",
        scatter_dimension=0,
        tiled=True,
    )
    w_second = a_second - update[blocks:] - correction
    l_second = couple(w_second, inv_d[1], inv_e[1], panel_pairs[1])
    return (l_first, l_second)


def solution(mesh):
    in_specs = (
        P("narrow", "wide"),
        P("narrow"),
        P("narrow"),
        P("narrow"),
        P(),
        P("narrow", "wide"),
        P("narrow", "wide"),
        P(None, "narrow"),
        P(None, "narrow"),
        P(None, "narrow"),
    )
    out_specs = (P("narrow", "wide"), P("narrow", "wide"))
    return jax.shard_map(shards, mesh=mesh, in_specs=in_specs, out_specs=out_specs, check_vma=False)
```

profile of v0, /device:TPU:0, one launch (start us, length us, event | category | flops | bytes accessed | tf_op | source)
XLA Modules:
  0.0 200.7 jit_solution(961543816702302315)
XLA Ops:
  7.2 0.0 all-gather.2.cloned.1.call-start
  7.2 0.7 broadcast_divide_fusion
  7.9 0.7 and_bitcast_fusion
  8.7 0.2 convert_reduce_fusion
  8.9 0.1 select_reduce_fusion
  9.1 0.1 fusion.2
  9.2 2.4 %copy.17 = f32[1024,768]{0,1:T(8,128)S(1)} copy(f32[1024,768]{1,0:T(8,128)} %param.10) | data formatting | bytes 6291456 | tf_op args[0]
  11.6 0.0 copy-start.7
  11.6 0.0 copy-start.8
  11.6 1.6 gather_fusion
  13.2 2.0 select_bitcast_fusion.1
  15.2 0.0 all-gather.2.cloned.1.call-update
  15.2 0.0 reduce-scatter.3.cloned.1.call-start
  15.3 0.0 copy-done.7
  15.3 0.0 copy-done.8
  15.3 0.1 pad_maximum_fusion
  15.4 75.4 %all-gather.2.cloned.1.call-done = f32[1024,1024]{0,1:T(8,128)} async-done(((f32[1024,128]{0,1:T(8,128)}), f32[1024,1024]{0,1:T(8,128)}) %all-gather.2.cloned.1.call-update) | async-done | bytes 4194320 | tf_op jit(solution)/shard_map/all_gather | solution.py:47
  90.9 5.0 %gather_fusion.1 = f32[512,1024]{1,0:T(8,128)S(1)} fusion(f32[1024,1024]{0,1:T(8,128)} %all-gather.2.cloned.1.call-done, s32[1024]{0:T(1024)S(1)} %pad_clamp_fusion.2), kind=kCustom, calls=%fused_computation.1 | custom fusion | bytes 4196352 | tf_op jit(solution)/shard_map/jit(_take)/gather | solution.py:48
  95.9 0.2 select_bitcast_fusion
  96.1 0.0 copy-start.6
  96.1 0.8 fusion.18
  96.9 0.0 copy-done.6
  97.0 0.8 multiply_add_fusion
  97.8 0.0 copy-start
  97.8 0.1 copy.18
  97.9 1.7 copy-done
  99.7 0.0 copy-start.5
  99.7 0.0 copy-start.9
  99.7 0.0 copy-start.10
  99.7 0.0 copy-start.11
  99.7 0.0 copy-start.3
  99.7 6.4 %fusion.21 = f32[512,768]{1,0:T(8,128)} fusion(f32[1024,512]{0,1:T(8,128)S(1)} %bitcast.68, f32[1024,768]{1,0:T(8,128)S(1)} %copy-done), kind=kOutput, calls=%fused_computation.83 | convolution fusion | flops 4831838208 | bytes 6815744 | tf_op jit(solution)/shard_map/dot_general | solution.py:57
  106.1 0.0 reduce-scatter.3.cloned.1.call-update
  106.1 0.0 reduce-scatter.5.cloned.1.call-start
  106.2 0.0 copy-done.5
  106.3 0.0 copy-done.9
  106.3 0.0 copy-done.10
  106.3 0.1 pad_maximum_fusion.2
  106.4 0.2 convert_reduce_fusion.1
  106.6 0.1 select_reduce_fusion.1
  106.8 0.1 fusion.8
  106.9 0.0 copy-done.11
  106.9 25.9 %reduce-scatter.3.cloned.1.call-done = f32[128,768]{1,0:T(8,128)} async-done(((f32[512,768]{1,0:T(8,128)}), f32[128,768]{1,0:T(8,128)}) %reduce-scatter.3.cloned.1.call-update) | async-done | bytes 393232 | tf_op jit(solution)/shard_map/reduce_scatter | solution.py:56
  132.9 0.0 copy-done.3
  132.9 0.9 slice_subtract_fusion.1
  133.9 0.1 multiply_add_fusion.2
  134.0 0.0 copy-start.1
  134.0 0.0 copy-start.2
  134.0 0.0 copy-start.4
  134.0 0.2 copy.19
  134.2 0.6 gather_fusion.2
  134.8 0.1 select_bitcast_fusion.2
  134.9 31.5 %all_gather.7 = f32[64,1024]{0,1:T(8,128)S(1)} all-gather(f32[64,128]{0,1:T(8,128)S(1)} %select_bitcast_fusion.2), channel_id=1, replica_groups=mesh['wide'=8,'narrow'=4] {'wide'}, dimensions={1}, use_global_device_ids=true | all-gather | bytes 294912 | tf_op jit(solution)/shard_map/all_gather | solution.py:68
  166.4 0.7 gather_fusion.3
  167.2 1.7 fusion.5
  168.9 0.0 reduce-scatter.5.cloned.1.call-update
  168.9 0.1 pad_maximum_fusion.1
  169.0 23.3 %reduce-scatter.5.cloned.1.call-done = f32[64,768]{1,0:T(8,128)} async-done(((f32[256,768]{1,0:T(8,128)}), f32[64,768]{1,0:T(8,128)}) %reduce-scatter.5.cloned.1.call-update) | async-done | bytes 196624 | tf_op jit(solution)/shard_map/reduce_scatter | solution.py:71
  192.3 0.0 copy-done.2
  192.3 0.0 copy-done.4
  192.3 1.0 fusion.4
  193.3 0.0 copy-done.1
  193.3 0.8 multiply_add_fusion.1
  (30 shorter events, 0.3 us)
Async XLA Ops:
  7.2 83.7 %all-gather.2.cloned.1.call-start = ((), (), s32[]{:S(2)}) async-start(), calls=%async_computation.2 | async-start | bytes 4718592 | tf_op jit(solution)/shard_map/all_gather | solution.py:47
  11.6 3.7 %copy-start.7 = (f32[1024]{0:T(1024)S(1)}, f32[1024]{0:T(1024)}, u32[]{:S(2)}) copy-start(f32[1024]{0:T(1024)} %param.12) | copy-start | bytes 12292
  11.6 3.7 %copy-start.8 = (s32[1024]{0:T(1024)S(1)}, s32[1024]{0:T(1024)}, u32[]{:S(2)}) copy-start(s32[1024]{0:T(1024)} %param.13) | copy-start | bytes 12292
  15.2 117.7 %reduce-scatter.3.cloned.1.call-start = ((), (), s32[]{:S(2)}) async-start(), calls=%async_computation.3 | async-start | bytes 1966080 | tf_op jit(solution)/shard_map/reduce_scatter | solution.py:56
  96.1 0.9 copy-start.6
  97.8 1.9 copy-start
  99.7 6.5 %copy-start.5 = (s32[2,256]{1,0:T(2,128)S(1)}, s32[2,256]{1,0:T(2,128)}, u32[]{:S(2)}) copy-start(s32[2,256]{1,0:T(2,128)} %param.14) | copy-start | bytes 6148
  99.7 6.6 %copy-start.9 = (s32[2,64]{1,0:T(2,128)S(1)}, s32[2,64]{1,0:T(2,128)}, u32[]{:S(2)}) copy-start(s32[2,64]{1,0:T(2,128)} %param.19) | copy-start | bytes 1540
  99.7 6.6 %copy-start.10 = (f32[2,64]{1,0:T(2,128)S(1)}, f32[2,64]{1,0:T(2,128)}, u32[]{:S(2)}) copy-start(f32[2,64]{1,0:T(2,128)} %param.18) | copy-start | bytes 1540
  99.7 7.2 %copy-start.11 = (f32[2,64]{1,0:T(2,128)S(1)}, f32[2,64]{1,0:T(2,128)}, u32[]{:S(2)}) copy-start(f32[2,64]{1,0:T(2,128)} %param.17) | copy-start | bytes 1540
  99.7 33.2 %copy-start.3 = (f32[64,768]{1,0:T(8,128)S(1)}, f32[64,768]{1,0:T(8,128)}, u32[]{:S(2)}) copy-start(f32[64,768]{1,0:T(8,128)} %param.15) | copy-start | bytes 589828
  106.1 86.2 %reduce-scatter.5.cloned.1.call-start = ((), (), s32[]{:S(2)}) async-start(), calls=%async_computation.4 | async-start | bytes 983040 | tf_op jit(solution)/shard_map/reduce_scatter | solution.py:71
  134.0 59.3 %copy-start.1 = (f32[64,768]{1,0:T(8,128)}, f32[64,768]{1,0:T(8,128)S(1)}, u32[]{:S(2)}) copy-start(f32[64,768]{1,0:T(8,128)S(1)} %multiply_add_fusion.2) | copy-start | bytes 589828
  134.0 58.3 %copy-start.2 = (f32[128,768]{1,0:T(8,128)S(1)}, f32[128,768]{1,0:T(8,128)}, u32[]{:S(2)}) copy-start(f32[128,768]{1,0:T(8,128)} %reduce-scatter.3.cloned.1.call-done) | copy-start | bytes 1179652
  134.0 58.3 %copy-start.4 = (f32[64,768]{1,0:T(8,128)S(1)}, f32[64,768]{1,0:T(8,128)}, u32[]{:S(2)}) copy-start(f32[64,768]{1,0:T(8,128)} %param.16) | copy-start | bytes 589828
Sparse Core Ops, SparseCore 0:
  15.3 75.5 all-gather.1
  106.3 26.5 reduce-scatter.2
  169.0 23.2 reduce-scatter.4
where the time goes:
time: 201 us
  waiting for transfers between devices  125 us (62%)
  blocking collectives  31.5 us (16%)
  between operations  14.1 us (7%)
  local copies, waits for them, and re-layouts  13.4 us (7%)
  other arithmetic  8.62 us (4%)
  matrix products  8.14 us (4%)
    all_gather x1, waiting for transfers between devices, shards(): gathered = lax.all_gather(packed, 'wide', axis=1, tiled=True)  75.4 us
    all_gather x1, blocking collectives, shards(): gathered_two = lax.all_gather(packed_two, 'wide', axis=1, tiled=True)  31.5 us
    reduce_scatter x1, waiting for transfers between devices, shards(): lax.psum_scatter(lax.dot_general(columns, prior_lt, (((0,), (0,)), ((), (...  25.9 us
    reduce_scatter x1, waiting for transfers between devices, shards(): lax.psum_scatter(lax.dot_general(columns, w_first, (((0,), (0,)), ((), ()...  23.3 us
    dot_general x1, matrix products, shards(): lax.dot_general(columns, prior_lt, (((0,), (0,)), ((), ())), precision=la...  6.42 us
    gather x1, local copies, waits for them, and re-layouts, shards(): chosen = jnp.take(gathered, slot, axis=1)  5.01 us
    unnamed x29, local copies, waits for them, and re-layouts  4.19 us
  transfers between devices with their start and end apart: 3, of which 3 were waited for; matrix products, arithmetic and copies ran while one was open for 0% of the time, Pallas kernels for 0%

commit v1 on v0

--- a/solution.py
+++ b/solution.py
@@ -65,7 +65,12 @@
     l_first = couple(w_first, inv_d[0], inv_e[0], panel_pairs[0])
     owner_two, rank_two, slot_two = slot_layout(second, tile_rows, capacity)
     packed_two = pack_local(l_first, second, owner_two, rank_two, here, tile_rows, capacity)
-    gathered_two = lax.all_gather(packed_two, "wide", axis=1, tiled=True)
+    ring = [packed_two]
+    for hop in range(7):
+        ring.append(lax.ppermute(ring[-1], "wide", [(dev, (dev + 1) % 8) for dev in range(8)]))
+    gathered_two = jnp.roll(
+        jnp.concatenate(ring[::-1], axis=1), (lax.axis_index("wide") + 1) * ring[0].shape[1], axis=1
+    )
     crossed = jnp.take(gathered_two, slot_two, axis=1)
     columns = crossed
     correction = lax.psum_scatter(

time: 201 us -> 217 us (1.080)
  waiting for transfers between devices: 125 us -> 169 us
  blocking collectives: 31.5 us -> 0 us
    ppermute x0 -> x7, waiting for transfers between devices: none -> 47.8 us  [shards(): lax.ppermute(ring[-1], 'wide', [(dev, (dev + 1) % 8) for dev in range(8)])]
    all_gather x1 -> x0, blocking collectives: 31.5 us -> none  [shards(): gathered_two = lax.all_gather(packed_two, 'wide', axis=1, tiled=True)]
    reduce_scatter x1, waiting for transfers between devices: 23.3 us -> 19.4 us  [shards(): lax.psum_scatter(lax.dot_general(columns, w_first, (((0,), (0,)), ((), ()...]
  transfers between devices with their start and end apart: 3 -> 10, of which waited for: 3 -> 10; matrix products, arithmetic and copies ran while one was open for 0% -> 0% of each run, Pallas kernels for 0% -> 0%
where the time goes in v1:
time: 217 us
  waiting for transfers between devices  169 us (78%)
  between operations  14.3 us (7%)
  local copies, waits for them, and re-layouts  13.5 us (6%)
  other arithmetic  10.2 us (5%)
  matrix products  8.12 us (4%)
    all_gather x1, waiting for transfers between devices, shards(): gathered = lax.all_gather(packed, 'wide', axis=1, tiled=True)  75.4 us
    ppermute x7, waiting for transfers between devices, shards(): lax.ppermute(ring[-1], 'wide', [(dev, (dev + 1) % 8) for dev in range(8)])  47.8 us
    reduce_scatter x1, waiting for transfers between devices, shards(): lax.psum_scatter(lax.dot_general(columns, prior_lt, (((0,), (0,)), ((), (...  26.4 us
    reduce_scatter x1, waiting for transfers between devices, shards(): lax.psum_scatter(lax.dot_general(columns, w_first, (((0,), (0,)), ((), ()...  19.4 us
    dot_general x1, matrix products, shards(): lax.dot_general(columns, prior_lt, (((0,), (0,)), ((), ())), precision=la...  6.41 us
    gather x1, local copies, waits for them, and re-layouts, shards(): chosen = jnp.take(gathered, slot, axis=1)  5.01 us
  transfers between devices with their start and end apart: 10, of which 10 were waited for; matrix products, arithmetic and copies ran while one was open for 0% of the time, Pallas kernels for 0%

profile of v1, /device:TPU:0, one launch (start us, length us, event | category | flops | bytes accessed | tf_op | source)
XLA Modules:
  0.0 216.8 jit_solution(5872956812041997501)
XLA Ops:
  7.2 0.0 all-gather.2.cloned.1.call-start
  7.2 0.7 and_select_fusion
  7.9 0.7 broadcast_divide_fusion
  8.6 0.7 and_bitcast_fusion
  9.3 0.7 compare_reduce_fusion
  10.1 0.2 convert_reduce_fusion
  10.3 0.1 select_reduce_fusion
  10.5 0.1 fusion.2
  10.7 0.2 convert_reduce_fusion.1
  10.8 0.1 select_reduce_fusion.1
  11.0 2.4 %copy.17 = f32[1024,768]{0,1:T(8,128)S(1)} copy(f32[1024,768]{1,0:T(8,128)} %param.10) | data formatting | bytes 6291456 | tf_op args[0]
  13.4 0.0 copy-start.6
  13.4 0.0 copy-start.7
  13.4 1.6 gather_fusion
  15.0 2.0 select_bitcast_fusion.1
  17.0 0.0 all-gather.2.cloned.1.call-update
  17.0 0.0 reduce-scatter.3.cloned.1.call-start
  17.1 0.1 pad_maximum_fusion
  17.2 75.4 %all-gather.2.cloned.1.call-done = f32[1024,1024]{0,1:T(8,128)} async-done(((f32[1024,128]{0,1:T(8,128)}), f32[1024,1024]{0,1:T(8,128)}) %all-gather.2.cloned.1.call-update) | async-done | bytes 4194320 | tf_op jit(solution)/shard_map/all_gather | solution.py:47
  92.7 5.0 %gather_fusion.1 = f32[512,1024]{1,0:T(8,128)S(1)} fusion(f32[1024,1024]{0,1:T(8,128)} %all-gather.2.cloned.1.call-done, s32[1024]{0:T(1024)S(1)} %pad_clamp_fusion.2), kind=kCustom, calls=%fused_computation.1 | custom fusion | bytes 4196352 | tf_op jit(solution)/shard_map/jit(_take)/gather | solution.py:48
  97.7 0.2 select_bitcast_fusion
  97.9 0.0 copy-start.5
  97.9 0.8 fusion.18
  98.7 0.0 copy-done.5
  98.7 0.8 multiply_add_fusion
  99.6 0.0 copy-start
  99.6 0.1 copy.18
  99.7 1.7 copy-done
  101.5 6.4 %fusion.21 = f32[512,768]{1,0:T(8,128)} fusion(f32[1024,512]{0,1:T(8,128)S(1)} %bitcast.72, f32[1024,768]{1,0:T(8,128)S(1)} %copy-done), kind=kOutput, calls=%fused_computation.100 | convolution fusion | flops 4831838208 | bytes 6815744 | tf_op jit(solution)/shard_map/dot_general | solution.py:57
  107.9 0.0 reduce-scatter.3.cloned.1.call-update
  107.9 0.0 reduce-scatter.5.cloned.1.call-start
  108.0 0.1 pad_maximum_fusion.2
  108.1 0.1 fusion.8
  108.2 26.4 %reduce-scatter.3.cloned.1.call-done = f32[128,768]{1,0:T(8,128)} async-done(((f32[512,768]{1,0:T(8,128)}), f32[128,768]{1,0:T(8,128)}) %reduce-scatter.3.cloned.1.call-update) | async-done | bytes 393232 | tf_op jit(solution)/shard_map/reduce_scatter | solution.py:56
  134.6 0.9 slice_subtract_fusion.1
  135.6 0.1 multiply_add_fusion.2
  135.7 0.0 copy-start.1
  135.7 0.2 copy.19
  135.9 0.6 gather_fusion.2
  136.5 0.1 select_bitcast_fusion.2
  136.6 1.5 collective-permute-start
  138.2 5.5 %collective-permute-done = f32[64,128]{0,1:T(8,128)S(1)} collective-permute-done((f32[64,128]{0,1:T(8,128)S(1)}, f32[64,128]{0,1:T(8,128)S(1)}, u32[]{:S(2)}, u32[]{:S(2)}) %collective-permute-start) | collective-permute-done | bytes 32800 | tf_op jit(solution)/shard_map/ppermute | solution.py:70
  143.7 0.0 collective-permute-start.1
  143.7 7.0 %collective-permute-done.1 = f32[64,128]{0,1:T(8,128)S(1)} collective-permute-done((f32[64,128]{0,1:T(8,128)S(1)}, f32[64,128]{0,1:T(8,128)S(1)}, u32[]{:S(2)}, u32[]{:S(2)}) %collective-permute-start.1) | collective-permute-done | bytes 32800 | tf_op jit(solution)/shard_map/ppermute | solution.py:70
  150.6 0.0 collective-permute-start.2
  150.6 7.0 %collective-permute-done.2 = f32[64,128]{0,1:T(8,128)S(1)} collective-permute-done((f32[64,128]{0,1:T(8,128)S(1)}, f32[64,128]{0,1:T(8,128)S(1)}, u32[]{:S(2)}, u32[]{:S(2)}) %collective-permute-start.2) | collective-permute-done | bytes 32800 | tf_op jit(solution)/shard_map/ppermute | solution.py:70
  157.6 0.0 collective-permute-start.3
  157.6 7.0 %collective-permute-done.3 = f32[64,128]{0,1:T(8,128)S(1)} collective-permute-done((f32[64,128]{0,1:T(8,128)S(1)}, f32[64,128]{0,1:T(8,128)S(1)}, u32[]{:S(2)}, u32[]{:S(2)}) %collective-permute-start.3) | collective-permute-done | bytes 32800 | tf_op jit(solution)/shard_map/ppermute | solution.py:70
  164.5 0.0 collective-permute-start.4
  164.6 7.6 %collective-permute-done.4 = f32[64,128]{0,1:T(8,128)S(1)} collective-permute-done((f32[64,128]{0,1:T(8,128)S(1)}, f32[64,128]{0,1:T(8,128)S(1)}, u32[]{:S(2)}, u32[]{:S(2)}) %collective-permute-start.4) | collective-permute-done | bytes 32800 | tf_op jit(solution)/shard_map/ppermute | solution.py:70
  172.1 0.0 collective-permute-start.5
  172.1 6.9 %collective-permute-done.5 = f32[64,128]{0,1:T(8,128)S(1)} collective-permute-done((f32[64,128]{0,1:T(8,128)S(1)}, f32[64,128]{0,1:T(8,128)S(1)}, u32[]{:S(2)}, u32[]{:S(2)}) %collective-permute-start.5) | collective-permute-done | bytes 32800 | tf_op jit(solution)/shard_map/ppermute | solution.py:70
  179.1 0.0 collective-permute-start.6
  179.1 6.9 %collective-permute-done.6 = f32[64,128]{0,1:T(8,128)S(1)} collective-permute-done((f32[64,128]{0,1:T(8,128)S(1)}, f32[64,128]{0,1:T(8,128)S(1)}, u32[]{:S(2)}, u32[]{:S(2)}) %collective-permute-start.6) | collective-permute-done | bytes 32800 | tf_op jit(solution)/shard_map/ppermute | solution.py:70
  186.1 0.1 constant_dynamic-update-slice_fusion.8
  186.3 0.0 copy-start.4
  186.4 0.1 constant_dynamic-update-slice_fusion
  186.5 0.7 gather_fusion.3
  187.3 1.7 fusion.5
  189.0 0.0 reduce-scatter.5.cloned.1.call-update
  189.0 0.1 pad_maximum_fusion.1
  189.1 19.4 %reduce-scatter.5.cloned.1.call-done = f32[64,768]{1,0:T(8,128)} async-done(((f32[256,768]{1,0:T(8,128)}), f32[64,768]{1,0:T(8,128)}) %reduce-scatter.5.cloned.1.call-update) | async-done | bytes 196624 | tf_op jit(solution)/shard_map/reduce_scatter | solution.py:76
  208.5 1.0 fusion.4
  209.5 0.8 multiply_add_fusion.1
  (56 shorter events, 0.4 us)
Async XLA Ops:
  7.2 85.5 %all-gather.2.cloned.1.call-start = ((), (), s32[]{:S(2)}) async-start(), calls=%async_computation.2 | async-start | bytes 4718592 | tf_op jit(solution)/shard_map/all_gather | solution.py:47
  13.4 3.7 %copy-start.6 = (f32[1024]{0:T(1024)S(1)}, f32[1024]{0:T(1024)}, u32[]{:S(2)}) copy-start(f32[1024]{0:T(1024)} %param.12) | copy-start | bytes 12292
  13.4 3.7 %copy-start.7 = (s32[1024]{0:T(1024)S(1)}, s32[1024]{0:T(1024)}, u32[]{:S(2)}) copy-start(s32[1024]{0:T(1024)} %param.13) | copy-start | bytes 12292
  17.0 117.6 %reduce-scatter.3.cloned.1.call-start = ((), (), s32[]{:S(2)}) async-start(), calls=%async_computation.3 | async-start | bytes 1966080 | tf_op jit(solution)/shard_map/reduce_scatter | solution.py:56
  97.9 0.9 copy-start.5
  99.6 1.9 copy-start
  101.5 6.5 %copy-start.8 = (s32[2,64]{1,0:T(2,128)S(1)}, s32[2,64]{1,0:T(2,128)}, u32[]{:S(2)}) copy-start(s32[2,64]{1,0:T(2,128)} %param.19) | copy-start | bytes 1540
  101.5 6.5 %copy-start.9 = (f32[2,64]{1,0:T(2,128)S(1)}, f32[2,64]{1,0:T(2,128)}, u32[]{:S(2)}) copy-start(f32[2,64]{1,0:T(2,128)} %param.18) | copy-start | bytes 1540
  101.5 6.7 %copy-start.10 = (f32[2,64]{1,0:T(2,128)S(1)}, f32[2,64]{1,0:T(2,128)}, u32[]{:S(2)}) copy-start(f32[2,64]{1,0:T(2,128)} %param.17) | copy-start | bytes 1540
  101.5 33.1 %copy-start.3 = (f32[64,768]{1,0:T(8,128)S(1)}, f32[64,768]{1,0:T(8,128)}, u32[]{:S(2)}) copy-start(f32[64,768]{1,0:T(8,128)} %param.15) | copy-start | bytes 589828
  107.9 100.6 %reduce-scatter.5.cloned.1.call-start = ((), (), s32[]{:S(2)}) async-start(), calls=%async_computation.4 | async-start | bytes 983040 | tf_op jit(solution)/shard_map/reduce_scatter | solution.py:76
  135.7 50.8 %copy-start.1 = (f32[64,768]{1,0:T(8,128)}, f32[64,768]{1,0:T(8,128)S(1)}, u32[]{:S(2)}) copy-start(f32[64,768]{1,0:T(8,128)S(1)} %multiply_add_fusion.2) | copy-start | bytes 589828
  136.6 7.0 %collective-permute-start = (f32[64,128]{0,1:T(8,128)S(1)}, f32[64,128]{0,1:T(8,128)S(1)}, u32[]{:S(2)}, u32[]{:S(2)}) collective-permute-start(f32[64,128]{0,1:T(8,128)S(1)} %select_bitcast_fusion.2), channel_id=1, source_target_pairs={{0,4},{4,8},{8,12},{12,16},{16,20},{20,24},{24,28},{28,0},{1,5},{5... | collective-permute-start | bytes 98312 | tf_op jit(solution)/shard_map/ppermute | solution.py:70
  143.7 7.0 %collective-permute-start.1 = (f32[64,128]{0,1:T(8,128)S(1)}, f32[64,128]{0,1:T(8,128)S(1)}, u32[]{:S(2)}, u32[]{:S(2)}) collective-permute-start(f32[64,128]{0,1:T(8,128)S(1)} %collective-permute-done), channel_id=1, source_target_pairs={{0,4},{4,8},{8,12},{12,16},{16,20},{20,24},{24,28},{28,0},{1,5},{5... | collective-permute-start | bytes 98312 | tf_op jit(solution)/shard_map/ppermute | solution.py:70
  150.6 7.0 %collective-permute-start.2 = (f32[64,128]{0,1:T(8,128)S(1)}, f32[64,128]{0,1:T(8,128)S(1)}, u32[]{:S(2)}, u32[]{:S(2)}) collective-permute-start(f32[64,128]{0,1:T(8,128)S(1)} %collective-permute-done.1), channel_id=1, source_target_pairs={{0,4},{4,8},{8,12},{12,16},{16,20},{20,24},{24,28},{28,0},{1,5},{5... | collective-permute-start | bytes 98312 | tf_op jit(solution)/shard_map/ppermute | solution.py:70
  157.6 7.0 %collective-permute-start.3 = (f32[64,128]{0,1:T(8,128)S(1)}, f32[64,128]{0,1:T(8,128)S(1)}, u32[]{:S(2)}, u32[]{:S(2)}) collective-permute-start(f32[64,128]{0,1:T(8,128)S(1)} %collective-permute-done.2), channel_id=1, source_target_pairs={{0,4},{4,8},{8,12},{12,16},{16,20},{20,24},{24,28},{28,0},{1,5},{5... | collective-permute-start | bytes 98312 | tf_op jit(solution)/shard_map/ppermute | solution.py:70
  164.5 7.6 %collective-permute-start.4 = (f32[64,128]{0,1:T(8,128)S(1)}, f32[64,128]{0,1:T(8,128)S(1)}, u32[]{:S(2)}, u32[]{:S(2)}) collective-permute-start(f32[64,128]{0,1:T(8,128)S(1)} %collective-permute-done.3), channel_id=1, source_target_pairs={{0,4},{4,8},{8,12},{12,16},{16,20},{20,24},{24,28},{28,0},{1,5},{5... | collective-permute-start | bytes 98312 | tf_op jit(solution)/shard_map/ppermute | solution.py:70
  172.1 7.0 %collective-permute-start.5 = (f32[64,128]{0,1:T(8,128)S(1)}, f32[64,128]{0,1:T(8,128)S(1)}, u32[]{:S(2)}, u32[]{:S(2)}) collective-permute-start(f32[64,128]{0,1:T(8,128)S(1)} %collective-permute-done.4), channel_id=1, source_target_pairs={{0,4},{4,8},{8,12},{12,16},{16,20},{20,24},{24,28},{28,0},{1,5},{5... | collective-permute-start | bytes 98312 | tf_op jit(solution)/shard_map/ppermute | solution.py:70
  179.1 7.0 %collective-permute-start.6 = (f32[64,128]{0,1:T(8,128)S(1)}, f32[64,128]{0,1:T(8,128)S(1)}, u32[]{:S(2)}, u32[]{:S(2)}) collective-permute-start(f32[64,128]{0,1:T(8,128)S(1)} %collective-permute-done.5), channel_id=1, source_target_pairs={{0,4},{4,8},{8,12},{12,16},{16,20},{20,24},{24,28},{28,0},{1,5},{5... | collective-permute-start | bytes 98312 | tf_op jit(solution)/shard_map/ppermute | solution.py:70
  186.3 22.2 %copy-start.2 = (f32[128,768]{1,0:T(8,128)S(1)}, f32[128,768]{1,0:T(8,128)}, u32[]{:S(2)}) copy-start(f32[128,768]{1,0:T(8,128)} %reduce-scatter.3.cloned.1.call-done) | copy-start | bytes 1179652
  186.3 22.2 %copy-start.4 = (f32[64,768]{1,0:T(8,128)S(1)}, f32[64,768]{1,0:T(8,128)}, u32[]{:S(2)}) copy-start(f32[64,768]{1,0:T(8,128)} %param.16) | copy-start | bytes 589828
Sparse Core Ops, SparseCore 0:
  17.1 75.5 all-gather.1
  108.0 26.5 reduce-scatter.2
  189.1 19.3 reduce-scatter.4
